TPU v7x, 32 devices: a whole 2x2x4 slice. The times are simulated.
32 devices in a mesh: seg: 4 (over y, x), blk: 8 (over z, core).
Axes of the slice: x: 2, y: 2, z: 4, core: 2. Of those that a mesh axis runs over, the one named last changes fastest.
Arguments:
- psi_init: float32 [4, 128, 128, 128], P('seg', 'blk'), may hold values from -6 to 6
- env_left: bfloat16 [4, 48, 8, 128, 128], P('seg', 'blk'), may hold values from -0.5 to 0.5
- env_right: bfloat16 [4, 48, 8, 128, 128], P('seg', 'blk'), may hold values from -0.5 to 0.5
- coef: float32 [4, 48, 128], P('seg', 'blk'), may hold values from -1.25 to 1.25
- source: int32 [4, 48, 128], P('seg', 'blk'), may hold values from 0 to 127
- right_sector: int32 [4, 16, 8], P('seg'), may hold values from 0 to 7, each once within a row
- sector_sizes: int32 [4, 2, 8], P('seg'), may hold values from 32 to 128, as said below
- step_size: float32 [4], P('seg'), may hold values from 0.2 to 0.6
Outputs:
- psi: float32 [4, 128, 128, 128], P('seg', 'blk')
- energy: float32 [4], P('seg')
- density: float32 [4, 1024, 128], P('seg', 'blk')
Inputs may be any that keep to these rules, and one draw needn't show every extreme that they name: `sector_sizes`: in each row of 8 sizes one equals 128. `right_sector`: each row is a permutation of the sectors.
All inputs are finite; a program needn't handle non-finite values.
Results may differ from a plain program's by a relative error of at most 0.0018.
Values may be sent and summed in bfloat16 or wider, within the bound.
No kernel may reach another device: no remote copies, remote signals or barrier semaphores. Data moves between devices by JAX's collectives and lax.ppermute only.
A program may use at most 128 MiB of HBM per device.

v0:
```python
import jax
import jax.numpy as jnp
from jax import lax
from jax.sharding import PartitionSpec as P

NSEC = 8
BS = 128
P_SIZE = 16
ITERS = 3
NB = 128


def shifted_2(block, axis, distance):
    devices = range(lax.axis_size(axis))
    route = [(i - distance, i) for i in devices if i - distance in devices]
    return lax.ppermute(block, axis, route)


def block_mask(indices, sizes, right_flat):
    left_ids = indices % NSEC
    right_ids = jnp.take(right_flat, indices)
    positions = jnp.arange(BS, dtype=jnp.int32)
    row_live = positions[None, :] < jnp.take(sizes[0], left_ids)[:, None]
    col_live = positions[None, :] < jnp.take(sizes[1], right_ids)[:, None]
    return (row_live[:, :, None] & col_live[:, None, :]).astype(jnp.float32)


def apply_terms(full_bf, indices, left_env, right_env, weights, sources, right_flat):
    left_ids = indices % NSEC
    right_ids = jnp.take(right_flat, indices)

    def channel(accum, inputs):
        left_one, right_one, source_one, weight_one = inputs
        picked = jnp.take(full_bf, jnp.take(source_one, indices), axis=0)
        left_mats = jnp.take(left_one, left_ids, axis=0)
        middle = jnp.einsum(
            "nay,nyb->nab", left_mats, picked, preferred_element_type=jnp.float32
        ).astype(jnp.bfloat16)
        right_mats = jnp.take(right_one, right_ids, axis=0)
        result = jnp.einsum("nab,ncb->nac", middle, right_mats, preferred_element_type=jnp.float32)
        scaled = jnp.take(weight_one, indices)
        return (accum + scaled[:, None, None] * result, None)

    initial = jnp.zeros((indices.shape[0], BS, BS), jnp.float32)
    summed, _ = lax.scan(channel, initial, (left_env, right_env, sources, weights))
    return summed


def gram_parts(vector, indices, right_flat):
    left_ids = indices % NSEC
    right_ids = jnp.take(right_flat, indices)
    gram_left = jnp.einsum("nxb,nyb->nxy", vector, vector, precision=lax.Precision.HIGHEST)
    gram_right = jnp.einsum("nax,nay->nxy", vector, vector, precision=lax.Precision.HIGHEST)
    labels = jnp.arange(NSEC, dtype=jnp.int32)
    one_left = (left_ids[:, None] == labels[None, :]).astype(jnp.float32)
    one_right = (right_ids[:, None] == labels[None, :]).astype(jnp.float32)
    left_rho = jnp.einsum(
        "ns,nxy->sxy", one_left, gram_left, precision=lax.Precision.HIGHEST
    ).reshape(NSEC * BS, BS)
    right_rho = jnp.einsum(
        "ns,nxy->sxy", one_right, gram_right, precision=lax.Precision.HIGHEST
    ).reshape(NSEC * BS, BS)
    return (left_rho, right_rho)


def update_vector(current, applied, square_sum, cross_sum, image_sum, step_len, cells_total):
    quotient = cross_sum / square_sum
    new_norm = square_sum + step_len * step_len * (image_sum - quotient * quotient * square_sum)
    updated = (current - step_len * (applied - quotient * current)) * jnp.sqrt(
        cells_total / new_norm
    )
    return (updated, quotient)


def on_device(psi_init, env_left, env_right, coef, source, right_sector, sector_sizes, step_size):
    left_env = env_left[0]
    right_env = env_right[0]
    weights = coef[0]
    sources = source[0]
    right_flat = right_sector[0].reshape(NB)
    sizes = sector_sizes[0]
    step_len = step_size[0]
    own_count = psi_init.shape[1]
    cells_total = float(NB * BS * BS)
    own_ids = lax.axis_index("blk") * own_count + jnp.arange(own_count, dtype=jnp.int32)
    own_live = block_mask(own_ids, sizes, right_flat)
    current = psi_init[0] * own_live
    quotient = jnp.zeros((), jnp.float32)
    for iteration in range(ITERS):
        full_bf = lax.all_gather(current.astype(jnp.bfloat16), "blk", axis=0, tiled=True)

        def partial_terms(begin_row, row_count, full_bf=full_bf):
            indices = jnp.arange(row_count, dtype=jnp.int32)
            return apply_terms(full_bf, indices, left_env, right_env, weights, sources, right_flat)

        applied = (
            lax.psum_scatter(
                partial_terms(jnp.int32(0), own_count * lax.axis_size("blk")),
                "blk",
                scatter_dimension=0,
                tiled=True,
            )
            * own_live
        )
        square_sum, cross_sum, image_sum = lax.psum(
            (jnp.sum(current * current), jnp.sum(current * applied), jnp.sum(applied * applied)),
            "blk",
        )
        current, quotient = update_vector(
            current, applied, square_sum, cross_sum, image_sum, step_len, cells_total
        )
    left_part, right_part = gram_parts(current, own_ids, right_flat)
    left_rows, right_rows = (
        lax.psum_scatter(left_part, "blk", scatter_dimension=0, tiled=True),
        lax.psum_scatter(right_part, "blk", scatter_dimension=0, tiled=True),
    )
    shifted = shifted_2(right_rows, "seg", 1)
    density = (left_rows + shifted) / float(P_SIZE * BS)
    return (current[None], quotient.reshape(1), density[None])


def solution(mesh):
    in_specs = (
        P("seg", "blk", None, None),
        P("seg", "blk", None, None, None),
        P("seg", "blk", None, None, None),
        P("seg", "blk", None),
        P("seg", "blk", None),
        P("seg", None, None),
        P("seg", None, None),
        P("seg"),
    )
    out_specs = (P("seg", "blk", None, None), P("seg"), P("seg", "blk", None))
    return jax.shard_map(
        on_device, mesh=mesh, in_specs=in_specs, out_specs=out_specs, check_vma=False
    )
```

profile of v0, /device:TPU:0, one launch (start us, length us, event | category | flops | bytes accessed | tf_op | source)
XLA Modules:
  0.0 1026.9 jit_solution(6705878778556902143)
XLA Ops:
  16.2 47.1 %all-gather.4.cloned.1.call-done = bf16[128,128,128]{2,1,0:T(8,128)(2,1)} async-done(((bf16[16,128,128]{2,1,0:T(8,128)(2,1)}), bf16[128,128,128]{2,1,0:T(8,128)(2,1)}) %all-gather.4.cloned.1.call-update) | async-done | bytes 4194320 | tf_op jit(solution)/shard_map/all_gather | solution.py:90
  63.3 155.7 %while.36 = (s32[]{:T(128)}, f32[128,128,128]{2,1,0:T(8,128)}, f32[6,128]{1,0:T(8,128)S(1)}, bf16[6,8,128,128]{3,2,1,0:T(8,128)(2,1)S(1)}, s32[6,128]{1,0:T(8,12...) while((s32[]{:T(128)}, f32[128,128,128]{2,1,0:T(8,128)}, ...), condition=%wide.region_1.8_spmd.clone.clone, body=%wide.region_0.7_spmd.clone.clone.sunk | while | flops 1088431104 | bytes 55605632 | solution.py:45
  78.1 9.6 select_add_fusion.6
  102.6 11.4 %select_add_fusion.6 = f32[128,128,128]{2,1,0:T(8,128)} fusion(f32[128,128,128]{2,1,0:T(8,128)} %get-tuple-element.638, f32[128]{0:T(128)S(1)} %compare_select_fusion.30, pred[]{:T(512)S(6)} %compare.15, bf16[128,128,128]{2,1,0:T(8,128)(2,1)} %gather_fusion.1, pred[128]{0:T(512)(128)(4,1)S(1)} %get-tuple-element.592, ...), kind=kOutput, calls=%fused_computation.25.clone.1 | convolution fusion | flops 1088421888 | bytes 29361024 | tf_op jit(solution)/shard_map/while/body/eval_jaxpr/nab,ncb->nac/dot_general | solution.py:40
  128.8 11.4 %select_add_fusion.6 = f32[128,128,128]{2,1,0:T(8,128)} fusion(f32[128,128,128]{2,1,0:T(8,128)} %get-tuple-element.638, f32[128]{0:T(128)S(1)} %compare_select_fusion.30, pred[]{:T(512)S(6)} %compare.15, bf16[128,128,128]{2,1,0:T(8,128)(2,1)} %gather_fusion.1, pred[128]{0:T(512)(128)(4,1)S(1)} %get-tuple-element.592, ...), kind=kOutput, calls=%fused_computation.25.clone.1 | convolution fusion | flops 1088421888 | bytes 29361024 | tf_op jit(solution)/shard_map/while/body/eval_jaxpr/nab,ncb->nac/dot_general | solution.py:40
  155.1 11.4 %select_add_fusion.6 = f32[128,128,128]{2,1,0:T(8,128)} fusion(f32[128,128,128]{2,1,0:T(8,128)} %get-tuple-element.638, f32[128]{0:T(128)S(1)} %compare_select_fusion.30, pred[]{:T(512)S(6)} %compare.15, bf16[128,128,128]{2,1,0:T(8,128)(2,1)} %gather_fusion.1, pred[128]{0:T(512)(128)(4,1)S(1)} %get-tuple-element.592, ...), kind=kOutput, calls=%fused_computation.25.clone.1 | convolution fusion | flops 1088421888 | bytes 29361024 | tf_op jit(solution)/shard_map/while/body/eval_jaxpr/nab,ncb->nac/dot_general | solution.py:40
  181.4 11.4 %select_add_fusion.6 = f32[128,128,128]{2,1,0:T(8,128)} fusion(f32[128,128,128]{2,1,0:T(8,128)} %get-tuple-element.638, f32[128]{0:T(128)S(1)} %compare_select_fusion.30, pred[]{:T(512)S(6)} %compare.15, bf16[128,128,128]{2,1,0:T(8,128)(2,1)} %gather_fusion.1, pred[128]{0:T(512)(128)(4,1)S(1)} %get-tuple-element.592, ...), kind=kOutput, calls=%fused_computation.25.clone.1 | convolution fusion | flops 1088421888 | bytes 29361024 | tf_op jit(solution)/shard_map/while/body/eval_jaxpr/nab,ncb->nac/dot_general | solution.py:40
  207.6 11.4 %select_add_fusion.6 = f32[128,128,128]{2,1,0:T(8,128)} fusion(f32[128,128,128]{2,1,0:T(8,128)} %get-tuple-element.638, f32[128]{0:T(128)S(1)} %compare_select_fusion.30, pred[]{:T(512)S(6)} %compare.15, bf16[128,128,128]{2,1,0:T(8,128)(2,1)} %gather_fusion.1, pred[128]{0:T(512)(128)(4,1)S(1)} %get-tuple-element.592, ...), kind=kOutput, calls=%fused_computation.25.clone.1 | convolution fusion | flops 1088421888 | bytes 29361024 | tf_op jit(solution)/shard_map/while/body/eval_jaxpr/nab,ncb->nac/dot_general | solution.py:40
  219.8 87.7 %reduce-scatter.6.cloned.1.call-done = f32[16,128,128]{2,1,0:T(8,128)} async-done(((f32[128,128,128]{2,1,0:T(8,128)}), f32[16,128,128]{2,1,0:T(8,128)}) %reduce-scatter.6.cloned.1.call-update) | async-done | bytes 1048592 | tf_op jit(solution)/shard_map/reduce_scatter | solution.py:97
  309.7 14.3 %all-reduce.2 = (f32[]{:T(128)}, f32[]{:T(128)}, f32[]{:T(128)}) all-reduce(f32[]{:T(128)} %get-tuple-element.347, f32[]{:T(128)} %get-tuple-element.348, f32[]{:T(128)} %get-tuple-element.346), channel_id=1, replica_groups=mesh['seg'=4,'blk'=8] {'blk'}, use_global_device_ids=true, to_apply=%region_6.13 | all-reduce | flops 3 | bytes 24 | tf_op jit(solution)/shard_map/psum | solution.py:105
  329.9 45.3 %all-gather.6.cloned.1.call-done = bf16[128,128,128]{2,1,0:T(8,128)(2,1)} async-done(((bf16[16,128,128]{2,1,0:T(8,128)(2,1)}), bf16[128,128,128]{2,1,0:T(8,128)(2,1)}) %all-gather.6.cloned.1.call-update) | async-done | bytes 4194320 | tf_op jit(solution)/shard_map/all_gather | solution.py:90
  375.2 155.7 %while.37 = (s32[]{:T(128)}, f32[128,128,128]{2,1,0:T(8,128)}, f32[6,128]{1,0:T(8,128)S(1)}, bf16[6,8,128,128]{3,2,1,0:T(8,128)(2,1)S(1)}, s32[6,128]{1,0:T(8,12...) while((s32[]{:T(128)}, f32[128,128,128]{2,1,0:T(8,128)}, ...), condition=%wide.region_10.17_spmd.clone.clone, body=%wide.region_9.16_spmd.clone.clone.sunk | while | flops 1088431104 | bytes 55605632 | solution.py:45
  390.0 9.6 select_add_fusion.7
  414.5 11.4 %select_add_fusion.7 = f32[128,128,128]{2,1,0:T(8,128)} fusion(f32[128,128,128]{2,1,0:T(8,128)} %get-tuple-element.668, f32[128]{0:T(128)S(1)} %compare_select_fusion.32, pred[]{:T(512)S(6)} %compare.16, bf16[128,128,128]{2,1,0:T(8,128)(2,1)} %gather_fusion.6, pred[128]{0:T(512)(128)(4,1)S(1)} %get-tuple-element.607, ...), kind=kOutput, calls=%fused_computation.56.clone.1 | convolution fusion | flops 1088421888 | bytes 29361024 | tf_op jit(solution)/shard_map/while/body/eval_jaxpr/nab,ncb->nac/dot_general | solution.py:40
  440.7 11.4 %select_add_fusion.7 = f32[128,128,128]{2,1,0:T(8,128)} fusion(f32[128,128,128]{2,1,0:T(8,128)} %get-tuple-element.668, f32[128]{0:T(128)S(1)} %compare_select_fusion.32, pred[]{:T(512)S(6)} %compare.16, bf16[128,128,128]{2,1,0:T(8,128)(2,1)} %gather_fusion.6, pred[128]{0:T(512)(128)(4,1)S(1)} %get-tuple-element.607, ...), kind=kOutput, calls=%fused_computation.56.clone.1 | convolution fusion | flops 1088421888 | bytes 29361024 | tf_op jit(solution)/shard_map/while/body/eval_jaxpr/nab,ncb->nac/dot_general | solution.py:40
  467.0 11.4 %select_add_fusion.7 = f32[128,128,128]{2,1,0:T(8,128)} fusion(f32[128,128,128]{2,1,0:T(8,128)} %get-tuple-element.668, f32[128]{0:T(128)S(1)} %compare_select_fusion.32, pred[]{:T(512)S(6)} %compare.16, bf16[128,128,128]{2,1,0:T(8,128)(2,1)} %gather_fusion.6, pred[128]{0:T(512)(128)(4,1)S(1)} %get-tuple-element.607, ...), kind=kOutput, calls=%fused_computation.56.clone.1 | convolution fusion | flops 1088421888 | bytes 29361024 | tf_op jit(solution)/shard_map/while/body/eval_jaxpr/nab,ncb->nac/dot_general | solution.py:40
  493.2 11.4 %select_add_fusion.7 = f32[128,128,128]{2,1,0:T(8,128)} fusion(f32[128,128,128]{2,1,0:T(8,128)} %get-tuple-element.668, f32[128]{0:T(128)S(1)} %compare_select_fusion.32, pred[]{:T(512)S(6)} %compare.16, bf16[128,128,128]{2,1,0:T(8,128)(2,1)} %gather_fusion.6, pred[128]{0:T(512)(128)(4,1)S(1)} %get-tuple-element.607, ...), kind=kOutput, calls=%fused_computation.56.clone.1 | convolution fusion | flops 1088421888 | bytes 29361024 | tf_op jit(solution)/shard_map/while/body/eval_jaxpr/nab,ncb->nac/dot_general | solution.py:40
  519.5 11.4 %select_add_fusion.7 = f32[128,128,128]{2,1,0:T(8,128)} fusion(f32[128,128,128]{2,1,0:T(8,128)} %get-tuple-element.668, f32[128]{0:T(128)S(1)} %compare_select_fusion.32, pred[]{:T(512)S(6)} %compare.16, bf16[128,128,128]{2,1,0:T(8,128)(2,1)} %gather_fusion.6, pred[128]{0:T(512)(128)(4,1)S(1)} %get-tuple-element.607, ...), kind=kOutput, calls=%fused_computation.56.clone.1 | convolution fusion | flops 1088421888 | bytes 29361024 | tf_op jit(solution)/shard_map/while/body/eval_jaxpr/nab,ncb->nac/dot_general | solution.py:40
  530.9 88.4 %reduce-scatter.8.cloned.1.call-done = f32[16,128,128]{2,1,0:T(8,128)} async-done(((f32[128,128,128]{2,1,0:T(8,128)}), f32[16,128,128]{2,1,0:T(8,128)}) %reduce-scatter.8.cloned.1.call-update) | async-done | bytes 1048592 | tf_op jit(solution)/shard_map/reduce_scatter | solution.py:97
  621.5 14.3 %all-reduce.1 = (f32[]{:T(128)}, f32[]{:T(128)}, f32[]{:T(128)}) all-reduce(f32[]{:T(128)} %get-tuple-element.350, f32[]{:T(128)} %get-tuple-element.345, f32[]{:T(128)} %get-tuple-element.344), channel_id=1, replica_groups=mesh['seg'=4,'blk'=8] {'blk'}, use_global_device_ids=true, to_apply=%region_15.22 | all-reduce | flops 3 | bytes 24 | tf_op jit(solution)/shard_map/psum | solution.py:105
  641.8 45.1 %all-gather.8.cloned.1.call-done = bf16[128,128,128]{2,1,0:T(8,128)(2,1)} async-done(((bf16[16,128,128]{2,1,0:T(8,128)(2,1)}), bf16[128,128,128]{2,1,0:T(8,128)(2,1)}) %all-gather.8.cloned.1.call-update) | async-done | bytes 4194320 | tf_op jit(solution)/shard_map/all_gather | solution.py:90
  686.9 155.7 %while.38 = (s32[]{:T(128)}, f32[128,128,128]{2,1,0:T(8,128)}, f32[6,128]{1,0:T(8,128)S(1)}, bf16[6,8,128,128]{3,2,1,0:T(8,128)(2,1)S(1)}, s32[6,128]{1,0:T(8,12...) while((s32[]{:T(128)}, f32[128,128,128]{2,1,0:T(8,128)}, ...), condition=%wide.region_19.26_spmd.clone.clone, body=%wide.region_18.25_spmd.clone.clone.sunk | while | flops 1088431104 | bytes 55605632 | solution.py:45
  701.8 9.6 select_add_fusion.8
  726.2 11.4 %select_add_fusion.8 = f32[128,128,128]{2,1,0:T(8,128)} fusion(f32[128,128,128]{2,1,0:T(8,128)} %get-tuple-element.698, f32[128]{0:T(128)S(1)} %compare_select_fusion.34, pred[]{:T(512)S(6)} %compare.17, bf16[128,128,128]{2,1,0:T(8,128)(2,1)} %gather_fusion.11, pred[128]{0:T(512)(128)(4,1)S(1)} %get-tuple-element.622, ...), kind=kOutput, calls=%fused_computation.87.clone.1 | convolution fusion | flops 1088421888 | bytes 29361024 | tf_op jit(solution)/shard_map/while/body/eval_jaxpr/nab,ncb->nac/dot_general | solution.py:40
  752.5 11.4 %select_add_fusion.8 = f32[128,128,128]{2,1,0:T(8,128)} fusion(f32[128,128,128]{2,1,0:T(8,128)} %get-tuple-element.698, f32[128]{0:T(128)S(1)} %compare_select_fusion.34, pred[]{:T(512)S(6)} %compare.17, bf16[128,128,128]{2,1,0:T(8,128)(2,1)} %gather_fusion.11, pred[128]{0:T(512)(128)(4,1)S(1)} %get-tuple-element.622, ...), kind=kOutput, calls=%fused_computation.87.clone.1 | convolution fusion | flops 1088421888 | bytes 29361024 | tf_op jit(solution)/shard_map/while/body/eval_jaxpr/nab,ncb->nac/dot_general | solution.py:40
  778.7 11.4 %select_add_fusion.8 = f32[128,128,128]{2,1,0:T(8,128)} fusion(f32[128,128,128]{2,1,0:T(8,128)} %get-tuple-element.698, f32[128]{0:T(128)S(1)} %compare_select_fusion.34, pred[]{:T(512)S(6)} %compare.17, bf16[128,128,128]{2,1,0:T(8,128)(2,1)} %gather_fusion.11, pred[128]{0:T(512)(128)(4,1)S(1)} %get-tuple-element.622, ...), kind=kOutput, calls=%fused_computation.87.clone.1 | convolution fusion | flops 1088421888 | bytes 29361024 | tf_op jit(solution)/shard_map/while/body/eval_jaxpr/nab,ncb->nac/dot_general | solution.py:40
  805.0 11.4 %select_add_fusion.8 = f32[128,128,128]{2,1,0:T(8,128)} fusion(f32[128,128,128]{2,1,0:T(8,128)} %get-tuple-element.698, f32[128]{0:T(128)S(1)} %compare_select_fusion.34, pred[]{:T(512)S(6)} %compare.17, bf16[128,128,128]{2,1,0:T(8,128)(2,1)} %gather_fusion.11, pred[128]{0:T(512)(128)(4,1)S(1)} %get-tuple-element.622, ...), kind=kOutput, calls=%fused_computation.87.clone.1 | convolution fusion | flops 1088421888 | bytes 29361024 | tf_op jit(solution)/shard_map/while/body/eval_jaxpr/nab,ncb->nac/dot_general | solution.py:40
  831.2 11.4 %select_add_fusion.8 = f32[128,128,128]{2,1,0:T(8,128)} fusion(f32[128,128,128]{2,1,0:T(8,128)} %get-tuple-element.698, f32[128]{0:T(128)S(1)} %compare_select_fusion.34, pred[]{:T(512)S(6)} %compare.17, bf16[128,128,128]{2,1,0:T(8,128)(2,1)} %gather_fusion.11, pred[128]{0:T(512)(128)(4,1)S(1)} %get-tuple-element.622, ...), kind=kOutput, calls=%fused_computation.87.clone.1 | convolution fusion | flops 1088421888 | bytes 29361024 | tf_op jit(solution)/shard_map/while/body/eval_jaxpr/nab,ncb->nac/dot_general | solution.py:40
  842.7 88.4 %reduce-scatter.10.cloned.1.call-done = f32[16,128,128]{2,1,0:T(8,128)} async-done(((f32[128,128,128]{2,1,0:T(8,128)}), f32[16,128,128]{2,1,0:T(8,128)}) %reduce-scatter.10.cloned.1.call-update) | async-done | bytes 1048592 | tf_op jit(solution)/shard_map/reduce_scatter | solution.py:97
  933.2 14.3 %all-reduce = (f32[]{:T(128)}, f32[]{:T(128)}, f32[]{:T(128)}) all-reduce(f32[]{:T(128)} %get-tuple-element.349, f32[]{:T(128)} %get-tuple-element.343, f32[]{:T(128)} %get-tuple-element.342), channel_id=1, replica_groups=mesh['seg'=4,'blk'=8] {'blk'}, use_global_device_ids=true, to_apply=%region_24.31 | all-reduce | flops 3 | bytes 24 | tf_op jit(solution)/shard_map/psum | solution.py:105
  960.6 25.3 %reduce-scatter.14.cloned.1.call-done = f32[128,128]{1,0:T(8,128)} async-done(((f32[1024,128]{1,0:T(8,128)}), f32[128,128]{1,0:T(8,128)}) %reduce-scatter.14.cloned.1.call-update) | async-done | bytes 65552 | tf_op jit(solution)/shard_map/reduce_scatter | solution.py:115
  989.2 28.2 %reduce-scatter.12.cloned.1.call-done = f32[128,128]{1,0:T(8,128)} async-done(((f32[1024,128]{1,0:T(8,128)}), f32[128,128]{1,0:T(8,128)}) %reduce-scatter.12.cloned.1.call-update) | async-done | bytes 65552 | tf_op jit(solution)/shard_map/reduce_scatter | solution.py:114
  (375 shorter events, 301.3 us)
Async XLA Ops:
  7.2 56.1 %copy-start.1 = (bf16[1,6,8,128,128]{4,3,2,1,0:T(8,128)(2,1)S(1)}, bf16[1,6,8,128,128]{4,3,2,1,0:T(8,128)(2,1)}, u32[]{:S(2)}) copy-start(bf16[1,6,8,128,128]{4,3,2,1,0:T(8,128)(2,1)} %param.27) | copy-start | bytes 4718596
  7.2 56.1 %all-gather.4.cloned.1.call-start = ((), (), s32[]{:S(2)}) async-start(), calls=%async_computation.5 | async-start | bytes 4718592 | tf_op jit(solution)/shard_map/all_gather | solution.py:90
  9.6 53.7 %copy-start.4 = (s32[16]{0:T(128)}, s32[16]{0:T(128)S(1)}, u32[]{:S(2)}) copy-start(s32[16]{0:T(128)S(1)} %get-tuple-element.419) | copy-start | bytes 196
  13.5 294.0 %reduce-scatter.6.cloned.1.call-start = ((), (), s32[]{:S(2)}) async-start(), calls=%async_computation.6 | async-start | bytes 9437184 | tf_op jit(solution)/shard_map/reduce_scatter | solution.py:97
  219.0 88.5 %copy-start.3 = (f32[1,16,128,128]{3,2,1,0:T(8,128)S(1)}, f32[1,16,128,128]{3,2,1,0:T(8,128)}, u32[]{:S(2)}) copy-start(f32[1,16,128,128]{3,2,1,0:T(8,128)} %param.26) | copy-start | bytes 3145732
  219.0 156.1 %all-gather.6.cloned.1.call-start = ((), (), s32[]{:S(2)}) async-start(), calls=%async_computation.7 | async-start | bytes 4718592 | tf_op jit(solution)/shard_map/all_gather | solution.py:90
  329.8 289.6 %copy-start.2 = (f32[16,128,128]{2,1,0:T(8,128)}, f32[16,128,128]{2,1,0:T(8,128)S(1)}, u32[]{:S(2)}) copy-start(f32[16,128,128]{2,1,0:T(8,128)S(1)} %get-tuple-element.417) | copy-start | bytes 3145732
  329.8 289.5 %reduce-scatter.8.cloned.1.call-start = ((), (), s32[]{:S(2)}) async-start(), calls=%async_computation.8 | async-start | bytes 9437184 | tf_op jit(solution)/shard_map/reduce_scatter | solution.py:97
  530.9 156.0 %all-gather.8.cloned.1.call-start = ((), (), s32[]{:S(2)}) async-start(), calls=%async_computation.9 | async-start | bytes 4718592 | tf_op jit(solution)/shard_map/all_gather | solution.py:90
  641.6 289.5 %reduce-scatter.10.cloned.1.call-start = ((), (), s32[]{:S(2)}) async-start(), calls=%async_computation.10 | async-start | bytes 9437184 | tf_op jit(solution)/shard_map/reduce_scatter | solution.py:97
  842.6 143.2 %reduce-scatter.14.cloned.1.call-start = ((), (), s32[]{:S(2)}) async-start(), calls=%async_computation.12 | async-start | bytes 589824 | tf_op jit(solution)/shard_map/reduce_scatter | solution.py:115
  931.1 23.1 %copy-start.5 = (s32[16]{0:T(128)S(1)}, s32[16]{0:T(128)}, u32[]{:S(2)}) copy-start(s32[16]{0:T(128)} %copy-done.4) | copy-start | bytes 196
  952.4 6.2 copy-start
  956.2 61.3 %reduce-scatter.12.cloned.1.call-start = ((), (), s32[]{:S(2)}) async-start(), calls=%async_computation.11 | async-start | bytes 589824 | tf_op jit(solution)/shard_map/reduce_scatter | solution.py:114
  985.9 31.6 %collective-permute-start = (f32[128,128]{1,0:T(8,128)}, f32[128,128]{1,0:T(8,128)S(1)}, u32[]{:S(2)}, u32[]{:S(2)}) collective-permute-start(f32[128,128]{1,0:T(8,128)} %reduce-scatter.14.cloned.1.call-done), channel_id=1, source_target_pairs={{0,8},{8,16},{16,24},{1,9},{9,17},{17,25},{2,10},{10,18},{18,26},{... | collective-permute-start | bytes 196616 | tf_op jit(solution)/shard_map/ppermute | solution.py:16
Sparse Core Ops, SparseCore 0:
  13.6 49.5 all-gather.3
  219.2 88.3 reduce-scatter.5
  330.0 45.1 all-gather.5
  531.0 88.3 reduce-scatter.7
  641.7 45.1 all-gather.7
  842.8 88.3 reduce-scatter.9
  956.3 29.4 reduce-scatter.13
  988.1 29.2 reduce-scatter.11
where the time goes:
time: 1030 us
  waiting for transfers between devices  456 us (44%)
  local copies, waits for them, and re-layouts  273 us (27%)
  matrix products  206 us (20%)
  blocking collectives  42.9 us (4%)
  between operations  26.2 us (3%)
  other arithmetic  17.7 us (2%)
    reduce_scatter x3, waiting for transfers between devices, on_device(): lax.psum_scatter(partial_terms(jnp.int32(0), own_count * lax.axis_size('b...  265 us
    dot_general x18, matrix products, channel(): jnp.einsum('nab,ncb->nac', middle, right_mats, preferred_element_type=jnp...  199 us
    all_gather x3, waiting for transfers between devices, on_device(): lax.all_gather(current.astype(jnp.bfloat16), 'blk', axis=0, tiled=True)  137 us
    gather x36, local copies, waits for them, and re-layouts, channel(): picked = jnp.take(full_bf, jnp.take(source_one, indices), axis=0)  116 us
    gather x18, local copies, waits for them, and re-layouts, channel(): left_mats = jnp.take(left_one, left_ids, axis=0)  55 us
    gather x18, local copies, waits for them, and re-layouts, channel(): right_mats = jnp.take(right_one, right_ids, axis=0)  54.5 us
    psum x3, blocking collectives, on_device(): lax.psum((jnp.sum(current * current), jnp.sum(current * applied), jnp.sum...  42.9 us
    reduce_scatter x1, waiting for transfers between devices, on_device(): lax.psum_scatter(left_part, 'blk', scatter_dimension=0, tiled=True)  28.2 us
  transfers between devices with their start and end apart: 9, of which 8 were waited for; matrix products, arithmetic and copies ran while one was open for 1% of the time, Pallas kernels for 0%

commit v1 on v0

--- a/solution.py
+++ b/solution.py
@@ -87,7 +87,26 @@
     current = psi_init[0] * own_live
     quotient = jnp.zeros((), jnp.float32)
     for iteration in range(ITERS):
-        full_bf = lax.all_gather(current.astype(jnp.bfloat16), "blk", axis=0, tiled=True)
+        array = current.astype(jnp.bfloat16)
+        ways, here, lap = (lax.axis_size("blk"), lax.axis_index("blk"), array.shape[0])
+        lengths = [n * ways if d == 0 else n for d, n in enumerate(array.shape)]
+        full = lax.dynamic_update_slice_in_dim(
+            jnp.zeros(lengths, array.dtype), array, here * lap, axis=0
+        )
+        going_up = going_down = array
+        for far in range(1, ways // 2 + 1):
+            going_up = lax.ppermute(going_up, "blk", [(d, (d + 1) % ways) for d in range(ways)])
+            full = lax.dynamic_update_slice_in_dim(
+                full, going_up, (here - far) % ways * lap, axis=0
+            )
+            if 2 * far < ways:
+                going_down = lax.ppermute(
+                    going_down, "blk", [(d, (d - 1) % ways) for d in range(ways)]
+                )
+                full = lax.dynamic_update_slice_in_dim(
+                    full, going_down, (here + far) % ways * lap, axis=0
+                )
+        full_bf = full
 
         def partial_terms(begin_row, row_count, full_bf=full_bf):
             indices = jnp.arange(row_count, dtype=jnp.int32)

time: 1030 us -> 1050 us (1.019)
  waiting for transfers between devices: 456 us -> 406 us
  local copies, waits for them, and re-layouts: 273 us -> 315 us
  starting transfers between devices: 3.86 us -> 35.4 us
    all_gather x3 -> x0, waiting for transfers between devices: 137 us -> none  [on_device(): lax.all_gather(current.astype(jnp.bfloat16), 'blk', axis=0, tiled=True)]
    ppermute x0 -> x21, waiting for transfers between devices: none -> 85 us  [the longest x12 82 us: on_device(): lax.ppermute(going_up, 'blk', [(d, (d + 1) % ways) for d in range(ways)])]
    ppermute x0 -> x21, starting transfers between devices: none -> 31.8 us  [the longest x9 31.3 us: on_device(): lax.ppermute(going_down, 'blk', [(d, (d - 1) % ways) for d in range(ways)])]
    dynamic_update_slice x0 -> x21, local copies, waits for them, and re-layouts: none -> 31.5 us  [the longest x12 19.6 us: on_device(): lax.dynamic_update_slice_in_dim(full, going_up, (here - far) % ways * lap...]
  transfers between devices with their start and end apart: 9 -> 27, of which waited for: 8 -> 20; matrix products, arithmetic and copies ran while one was open for 1% -> 3% of each run, Pallas kernels for 0% -> 0%
where the time goes in v1:
time: 1050 us
  waiting for transfers between devices  406 us (39%)
  local copies, waits for them, and re-layouts  315 us (30%)
  matrix products  206 us (20%)
  blocking collectives  43.2 us (4%)
  starting transfers between devices  35.4 us (3%)
  between operations  26.1 us (2%)
  other arithmetic  14 us (1%)
    reduce_scatter x3, waiting for transfers between devices, on_device(): lax.psum_scatter(partial_terms(jnp.int32(0), own_count * lax.axis_size('b...  268 us
    dot_general x18, matrix products, channel(): jnp.einsum('nab,ncb->nac', middle, right_mats, preferred_element_type=jnp...  200 us
    gather x36, local copies, waits for them, and re-layouts, channel(): picked = jnp.take(full_bf, jnp.take(source_one, indices), axis=0)  116 us
    ppermute x12, waiting for transfers between devices, on_device(): lax.ppermute(going_up, 'blk', [(d, (d + 1) % ways) for d in range(ways)])  82 us
    gather x18, local copies, waits for them, and re-layouts, channel(): right_mats = jnp.take(right_one, right_ids, axis=0)  55.3 us
    gather x18, local copies, waits for them, and re-layouts, channel(): left_mats = jnp.take(left_one, left_ids, axis=0)  54.5 us
    psum x3, blocking collectives, on_device(): lax.psum((jnp.sum(current * current), jnp.sum(current * applied), jnp.sum...  43.2 us
    ppermute x9, starting transfers between devices, on_device(): lax.ppermute(going_down, 'blk', [(d, (d - 1) % ways) for d in range(ways)])  31.3 us
  transfers between devices with their start and end apart: 27, of which 20 were waited for; matrix products, arithmetic and copies ran while one was open for 3% of the time, Pallas kernels for 0%

profile of v1, /device:TPU:0, one launch (start us, length us, event | category | flops | bytes accessed | tf_op | source)
XLA Modules:
  0.0 1048.2 jit_solution(17981652777255554392)
XLA Ops:
  19.9 9.9 collective-permute-done
  66.0 156.2 %while.36 = (s32[]{:T(128)}, f32[128,128,128]{2,1,0:T(8,128)}, f32[6,128]{1,0:T(8,128)S(1)}, bf16[6,8,128,128]{3,2,1,0:T(8,128)(2,1)S(1)}, s32[6,128]{1,0:T(8,12...) while((s32[]{:T(128)}, f32[128,128,128]{2,1,0:T(8,128)}, ...), condition=%wide.region_1.8_spmd.clone.clone, body=%wide.region_0.7_spmd.clone.clone.sunk | while | flops 1088431104 | bytes 55605624 | solution.py:45
  80.9 9.6 select_add_fusion.6
  105.4 11.4 %select_add_fusion.6 = f32[128,128,128]{2,1,0:T(8,128)} fusion(f32[128,128,128]{2,1,0:T(8,128)} %get-tuple-element.642, f32[128]{0:T(128)S(1)} %compare_select_fusion.30, pred[]{:T(512)S(6)} %compare.22, bf16[128,128,128]{2,1,0:T(8,128)(2,1)} %gather_fusion.1, pred[128]{0:T(512)(128)(4,1)S(1)} %get-tuple-element.596, ...), kind=kOutput, calls=%fused_computation.25.clone.1 | convolution fusion | flops 1088421888 | bytes 29361024 | tf_op jit(solution)/shard_map/while/body/eval_jaxpr/nab,ncb->nac/dot_general | solution.py:40
  131.7 11.4 %select_add_fusion.6 = f32[128,128,128]{2,1,0:T(8,128)} fusion(f32[128,128,128]{2,1,0:T(8,128)} %get-tuple-element.642, f32[128]{0:T(128)S(1)} %compare_select_fusion.30, pred[]{:T(512)S(6)} %compare.22, bf16[128,128,128]{2,1,0:T(8,128)(2,1)} %gather_fusion.1, pred[128]{0:T(512)(128)(4,1)S(1)} %get-tuple-element.596, ...), kind=kOutput, calls=%fused_computation.25.clone.1 | convolution fusion | flops 1088421888 | bytes 29361024 | tf_op jit(solution)/shard_map/while/body/eval_jaxpr/nab,ncb->nac/dot_general | solution.py:40
  158.0 11.4 %select_add_fusion.6 = f32[128,128,128]{2,1,0:T(8,128)} fusion(f32[128,128,128]{2,1,0:T(8,128)} %get-tuple-element.642, f32[128]{0:T(128)S(1)} %compare_select_fusion.30, pred[]{:T(512)S(6)} %compare.22, bf16[128,128,128]{2,1,0:T(8,128)(2,1)} %gather_fusion.1, pred[128]{0:T(512)(128)(4,1)S(1)} %get-tuple-element.596, ...), kind=kOutput, calls=%fused_computation.25.clone.1 | convolution fusion | flops 1088421888 | bytes 29361024 | tf_op jit(solution)/shard_map/while/body/eval_jaxpr/nab,ncb->nac/dot_general | solution.py:40
  184.4 11.4 %select_add_fusion.6 = f32[128,128,128]{2,1,0:T(8,128)} fusion(f32[128,128,128]{2,1,0:T(8,128)} %get-tuple-element.642, f32[128]{0:T(128)S(1)} %compare_select_fusion.30, pred[]{:T(512)S(6)} %compare.22, bf16[128,128,128]{2,1,0:T(8,128)(2,1)} %gather_fusion.1, pred[128]{0:T(512)(128)(4,1)S(1)} %get-tuple-element.596, ...), kind=kOutput, calls=%fused_computation.25.clone.1 | convolution fusion | flops 1088421888 | bytes 29361024 | tf_op jit(solution)/shard_map/while/body/eval_jaxpr/nab,ncb->nac/dot_general | solution.py:40
  210.7 11.4 %select_add_fusion.6 = f32[128,128,128]{2,1,0:T(8,128)} fusion(f32[128,128,128]{2,1,0:T(8,128)} %get-tuple-element.642, f32[128]{0:T(128)S(1)} %compare_select_fusion.30, pred[]{:T(512)S(6)} %compare.22, bf16[128,128,128]{2,1,0:T(8,128)(2,1)} %gather_fusion.1, pred[128]{0:T(512)(128)(4,1)S(1)} %get-tuple-element.596, ...), kind=kOutput, calls=%fused_computation.25.clone.1 | convolution fusion | flops 1088421888 | bytes 29361024 | tf_op jit(solution)/shard_map/while/body/eval_jaxpr/nab,ncb->nac/dot_general | solution.py:40
  222.9 92.2 %reduce-scatter.6.cloned.1.call-done = f32[16,128,128]{2,1,0:T(8,128)} async-done(((f32[128,128,128]{2,1,0:T(8,128)}), f32[16,128,128]{2,1,0:T(8,128)}) %reduce-scatter.6.cloned.1.call-update) | async-done | bytes 1048592 | tf_op jit(solution)/shard_map/reduce_scatter | solution.py:116
  317.2 14.3 %all-reduce.2 = (f32[]{:T(128)}, f32[]{:T(128)}, f32[]{:T(128)}) all-reduce(f32[]{:T(128)} %get-tuple-element.347, f32[]{:T(128)} %get-tuple-element.348, f32[]{:T(128)} %get-tuple-element.346), channel_id=1, replica_groups=mesh['seg'=4,'blk'=8] {'blk'}, use_global_device_ids=true, to_apply=%region_6.13 | all-reduce | flops 3 | bytes 24 | tf_op jit(solution)/shard_map/psum | solution.py:124
  342.8 10.3 collective-permute-done.7
  389.8 156.2 %while.37 = (s32[]{:T(128)}, f32[128,128,128]{2,1,0:T(8,128)}, f32[6,128]{1,0:T(8,128)S(1)}, bf16[6,8,128,128]{3,2,1,0:T(8,128)(2,1)S(1)}, s32[6,128]{1,0:T(8,12...) while((s32[]{:T(128)}, f32[128,128,128]{2,1,0:T(8,128)}, ...), condition=%wide.region_10.17_spmd.clone.clone, body=%wide.region_9.16_spmd.clone.clone.sunk | while | flops 1088431104 | bytes 55605624 | solution.py:45
  404.7 9.6 select_add_fusion.7
  429.2 11.4 %select_add_fusion.7 = f32[128,128,128]{2,1,0:T(8,128)} fusion(f32[128,128,128]{2,1,0:T(8,128)} %get-tuple-element.672, f32[128]{0:T(128)S(1)} %compare_select_fusion.32, pred[]{:T(512)S(6)} %compare.23, bf16[128,128,128]{2,1,0:T(8,128)(2,1)} %gather_fusion.6, pred[128]{0:T(512)(128)(4,1)S(1)} %get-tuple-element.611, ...), kind=kOutput, calls=%fused_computation.56.clone.1 | convolution fusion | flops 1088421888 | bytes 29361024 | tf_op jit(solution)/shard_map/while/body/eval_jaxpr/nab,ncb->nac/dot_general | solution.py:40
  455.5 11.4 %select_add_fusion.7 = f32[128,128,128]{2,1,0:T(8,128)} fusion(f32[128,128,128]{2,1,0:T(8,128)} %get-tuple-element.672, f32[128]{0:T(128)S(1)} %compare_select_fusion.32, pred[]{:T(512)S(6)} %compare.23, bf16[128,128,128]{2,1,0:T(8,128)(2,1)} %gather_fusion.6, pred[128]{0:T(512)(128)(4,1)S(1)} %get-tuple-element.611, ...), kind=kOutput, calls=%fused_computation.56.clone.1 | convolution fusion | flops 1088421888 | bytes 29361024 | tf_op jit(solution)/shard_map/while/body/eval_jaxpr/nab,ncb->nac/dot_general | solution.py:40
  481.8 11.4 %select_add_fusion.7 = f32[128,128,128]{2,1,0:T(8,128)} fusion(f32[128,128,128]{2,1,0:T(8,128)} %get-tuple-element.672, f32[128]{0:T(128)S(1)} %compare_select_fusion.32, pred[]{:T(512)S(6)} %compare.23, bf16[128,128,128]{2,1,0:T(8,128)(2,1)} %gather_fusion.6, pred[128]{0:T(512)(128)(4,1)S(1)} %get-tuple-element.611, ...), kind=kOutput, calls=%fused_computation.56.clone.1 | convolution fusion | flops 1088421888 | bytes 29361024 | tf_op jit(solution)/shard_map/while/body/eval_jaxpr/nab,ncb->nac/dot_general | solution.py:40
  508.2 11.4 %select_add_fusion.7 = f32[128,128,128]{2,1,0:T(8,128)} fusion(f32[128,128,128]{2,1,0:T(8,128)} %get-tuple-element.672, f32[128]{0:T(128)S(1)} %compare_select_fusion.32, pred[]{:T(512)S(6)} %compare.23, bf16[128,128,128]{2,1,0:T(8,128)(2,1)} %gather_fusion.6, pred[128]{0:T(512)(128)(4,1)S(1)} %get-tuple-element.611, ...), kind=kOutput, calls=%fused_computation.56.clone.1 | convolution fusion | flops 1088421888 | bytes 29361024 | tf_op jit(solution)/shard_map/while/body/eval_jaxpr/nab,ncb->nac/dot_general | solution.py:40
  534.5 11.4 %select_add_fusion.7 = f32[128,128,128]{2,1,0:T(8,128)} fusion(f32[128,128,128]{2,1,0:T(8,128)} %get-tuple-element.672, f32[128]{0:T(128)S(1)} %compare_select_fusion.32, pred[]{:T(512)S(6)} %compare.23, bf16[128,128,128]{2,1,0:T(8,128)(2,1)} %gather_fusion.6, pred[128]{0:T(512)(128)(4,1)S(1)} %get-tuple-element.611, ...), kind=kOutput, calls=%fused_computation.56.clone.1 | convolution fusion | flops 1088421888 | bytes 29361024 | tf_op jit(solution)/shard_map/while/body/eval_jaxpr/nab,ncb->nac/dot_general | solution.py:40
  546.0 87.8 %reduce-scatter.8.cloned.1.call-done = f32[16,128,128]{2,1,0:T(8,128)} async-done(((f32[128,128,128]{2,1,0:T(8,128)}), f32[16,128,128]{2,1,0:T(8,128)}) %reduce-scatter.8.cloned.1.call-update) | async-done | bytes 1048592 | tf_op jit(solution)/shard_map/reduce_scatter | solution.py:116
  635.9 14.4 %all-reduce.1 = (f32[]{:T(128)}, f32[]{:T(128)}, f32[]{:T(128)}) all-reduce(f32[]{:T(128)} %get-tuple-element.350, f32[]{:T(128)} %get-tuple-element.345, f32[]{:T(128)} %get-tuple-element.344), channel_id=1, replica_groups=mesh['seg'=4,'blk'=8] {'blk'}, use_global_device_ids=true, to_apply=%region_15.22 | all-reduce | flops 3 | bytes 24 | tf_op jit(solution)/shard_map/psum | solution.py:124
  661.6 10.3 collective-permute-done.14
  708.6 156.2 %while.38 = (s32[]{:T(128)}, f32[128,128,128]{2,1,0:T(8,128)}, f32[6,128]{1,0:T(8,128)S(1)}, bf16[6,8,128,128]{3,2,1,0:T(8,128)(2,1)S(1)}, s32[6,128]{1,0:T(8,12...) while((s32[]{:T(128)}, f32[128,128,128]{2,1,0:T(8,128)}, ...), condition=%wide.region_19.26_spmd.clone.clone, body=%wide.region_18.25_spmd.clone.clone.sunk | while | flops 1088431104 | bytes 55605624 | solution.py:45
  723.5 9.6 select_add_fusion.8
  748.0 11.4 %select_add_fusion.8 = f32[128,128,128]{2,1,0:T(8,128)} fusion(f32[128,128,128]{2,1,0:T(8,128)} %get-tuple-element.702, f32[128]{0:T(128)S(1)} %compare_select_fusion.34, pred[]{:T(512)S(6)} %compare.24, bf16[128,128,128]{2,1,0:T(8,128)(2,1)} %gather_fusion.11, pred[128]{0:T(512)(128)(4,1)S(1)} %get-tuple-element.626, ...), kind=kOutput, calls=%fused_computation.87.clone.1 | convolution fusion | flops 1088421888 | bytes 29361024 | tf_op jit(solution)/shard_map/while/body/eval_jaxpr/nab,ncb->nac/dot_general | solution.py:40
  774.3 11.4 %select_add_fusion.8 = f32[128,128,128]{2,1,0:T(8,128)} fusion(f32[128,128,128]{2,1,0:T(8,128)} %get-tuple-element.702, f32[128]{0:T(128)S(1)} %compare_select_fusion.34, pred[]{:T(512)S(6)} %compare.24, bf16[128,128,128]{2,1,0:T(8,128)(2,1)} %gather_fusion.11, pred[128]{0:T(512)(128)(4,1)S(1)} %get-tuple-element.626, ...), kind=kOutput, calls=%fused_computation.87.clone.1 | convolution fusion | flops 1088421888 | bytes 29361024 | tf_op jit(solution)/shard_map/while/body/eval_jaxpr/nab,ncb->nac/dot_general | solution.py:40
  800.7 11.4 %select_add_fusion.8 = f32[128,128,128]{2,1,0:T(8,128)} fusion(f32[128,128,128]{2,1,0:T(8,128)} %get-tuple-element.702, f32[128]{0:T(128)S(1)} %compare_select_fusion.34, pred[]{:T(512)S(6)} %compare.24, bf16[128,128,128]{2,1,0:T(8,128)(2,1)} %gather_fusion.11, pred[128]{0:T(512)(128)(4,1)S(1)} %get-tuple-element.626, ...), kind=kOutput, calls=%fused_computation.87.clone.1 | convolution fusion | flops 1088421888 | bytes 29361024 | tf_op jit(solution)/shard_map/while/body/eval_jaxpr/nab,ncb->nac/dot_general | solution.py:40
  827.0 11.4 %select_add_fusion.8 = f32[128,128,128]{2,1,0:T(8,128)} fusion(f32[128,128,128]{2,1,0:T(8,128)} %get-tuple-element.702, f32[128]{0:T(128)S(1)} %compare_select_fusion.34, pred[]{:T(512)S(6)} %compare.24, bf16[128,128,128]{2,1,0:T(8,128)(2,1)} %gather_fusion.11, pred[128]{0:T(512)(128)(4,1)S(1)} %get-tuple-element.626, ...), kind=kOutput, calls=%fused_computation.87.clone.1 | convolution fusion | flops 1088421888 | bytes 29361024 | tf_op jit(solution)/shard_map/while/body/eval_jaxpr/nab,ncb->nac/dot_general | solution.py:40
  853.3 11.4 %select_add_fusion.8 = f32[128,128,128]{2,1,0:T(8,128)} fusion(f32[128,128,128]{2,1,0:T(8,128)} %get-tuple-element.702, f32[128]{0:T(128)S(1)} %compare_select_fusion.34, pred[]{:T(512)S(6)} %compare.24, bf16[128,128,128]{2,1,0:T(8,128)(2,1)} %gather_fusion.11, pred[128]{0:T(512)(128)(4,1)S(1)} %get-tuple-element.626, ...), kind=kOutput, calls=%fused_computation.87.clone.1 | convolution fusion | flops 1088421888 | bytes 29361024 | tf_op jit(solution)/shard_map/while/body/eval_jaxpr/nab,ncb->nac/dot_general | solution.py:40
  864.8 87.8 %reduce-scatter.10.cloned.1.call-done = f32[16,128,128]{2,1,0:T(8,128)} async-done(((f32[128,128,128]{2,1,0:T(8,128)}), f32[16,128,128]{2,1,0:T(8,128)}) %reduce-scatter.10.cloned.1.call-update) | async-done | bytes 1048592 | tf_op jit(solution)/shard_map/reduce_scatter | solution.py:116
  954.7 14.5 %all-reduce = (f32[]{:T(128)}, f32[]{:T(128)}, f32[]{:T(128)}) all-reduce(f32[]{:T(128)} %get-tuple-element.349, f32[]{:T(128)} %get-tuple-element.343, f32[]{:T(128)} %get-tuple-element.342), channel_id=1, replica_groups=mesh['seg'=4,'blk'=8] {'blk'}, use_global_device_ids=true, to_apply=%region_24.31 | all-reduce | flops 3 | bytes 24 | tf_op jit(solution)/shard_map/psum | solution.py:124
  982.3 25.2 %reduce-scatter.14.cloned.1.call-done = f32[128,128]{1,0:T(8,128)} async-done(((f32[1024,128]{1,0:T(8,128)}), f32[128,128]{1,0:T(8,128)}) %reduce-scatter.14.cloned.1.call-update) | async-done | bytes 65552 | tf_op jit(solution)/shard_map/reduce_scatter | solution.py:134
  1010.9 28.1 %reduce-scatter.12.cloned.1.call-done = f32[128,128]{1,0:T(8,128)} async-done(((f32[1024,128]{1,0:T(8,128)}), f32[128,128]{1,0:T(8,128)}) %reduce-scatter.12.cloned.1.call-update) | async-done | bytes 65552 | tf_op jit(solution)/shard_map/reduce_scatter | solution.py:133
  (450 shorter events, 425.5 us)
Async XLA Ops:
  7.2 307.9 %reduce-scatter.6.cloned.1.call-start = ((), (), s32[]{:S(2)}) async-start(), calls=%async_computation.5 | async-start | bytes 9437184 | tf_op jit(solution)/shard_map/reduce_scatter | solution.py:116
  8.8 34.9 %copy-start.11 = (s32[1,6,128]{2,0,1:T(1,128)S(1)}, s32[1,6,128]{2,0,1:T(1,128)}, u32[]{:S(2)}) copy-start(s32[1,6,128]{2,0,1:T(1,128)} %param.30) | copy-start | bytes 9220
  8.8 34.9 %copy-start.12 = (f32[1,6,128]{2,0,1:T(1,128)S(1)}, f32[1,6,128]{2,0,1:T(1,128)}, u32[]{:S(2)}) copy-start(f32[1,6,128]{2,0,1:T(1,128)} %param.29) | copy-start | bytes 9220
  15.4 50.6 %copy-start.1 = (bf16[1,6,8,128,128]{4,3,2,1,0:T(8,128)(2,1)S(1)}, bf16[1,6,8,128,128]{4,3,2,1,0:T(8,128)(2,1)}, u32[]{:S(2)}) copy-start(bf16[1,6,8,128,128]{4,3,2,1,0:T(8,128)(2,1)} %param.27) | copy-start | bytes 4718596
  15.4 14.5 %collective-permute-start = (bf16[16,128,128]{2,1,0:T(8,128)(2,1)S(1)}, bf16[16,128,128]{2,1,0:T(8,128)(2,1)S(1)}, u32[]{:S(2)}, u32[]{:S(2)}) collective-permute-start(bf16[16,128,128]{2,1,0:T(8,128)(2,1)S(1)} %get-tuple-element.421), channel_id=1, source_target_pairs={{0,1},{1,2},{2,3},{3,4},{4,5},{5,6},{6,7},{7,0},{8,9},{9,10},{10,1... | collective-permute-start | bytes 1572872 | tf_op jit(solution)/shard_map/ppermute | solution.py:98
  15.9 14.3 %collective-permute-start.1 = (bf16[16,128,128]{2,1,0:T(8,128)(2,1)S(1)}, bf16[16,128,128]{2,1,0:T(8,128)(2,1)}, u32[]{:S(2)}, u32[]{:S(2)}) collective-permute-start(bf16[16,128,128]{2,1,0:T(8,128)(2,1)S(1)} %get-tuple-element.421), channel_id=1, source_target_pairs={{0,7},{1,0},{2,1},{3,2},{4,3},{5,4},{6,5},{7,6},{8,15},{9,8},{10,9... | collective-permute-start | bytes 1572872 | tf_op jit(solution)/shard_map/ppermute | solution.py:103
  29.9 12.6 %collective-permute-start.2 = (bf16[16,128,128]{2,1,0:T(8,128)(2,1)S(1)}, bf16[16,128,128]{2,1,0:T(8,128)(2,1)}, u32[]{:S(2)}, u32[]{:S(2)}) collective-permute-start(bf16[16,128,128]{2,1,0:T(8,128)(2,1)S(1)} %collective-permute-done), channel_id=1, source_target_pairs={{0,1},{1,2},{2,3},{3,4},{4,5},{5,6},{6,7},{7,0},{8,9},{9,10},{10,1... | collective-permute-start | bytes 1572872 | tf_op jit(solution)/shard_map/ppermute | solution.py:98
  30.6 13.1 %collective-permute-start.3 = (bf16[16,128,128]{2,1,0:T(8,128)(2,1)}, bf16[16,128,128]{2,1,0:T(8,128)(2,1)}, u32[]{:S(2)}, u32[]{:S(2)}) collective-permute-start(bf16[16,128,128]{2,1,0:T(8,128)(2,1)} %collective-permute-done.1), channel_id=1, source_target_pairs={{0,7},{1,0},{2,1},{3,2},{4,3},{5,4},{6,5},{7,6},{8,15},{9,8},{10,9... | collective-permute-start | bytes 1572872 | tf_op jit(solution)/shard_map/ppermute | solution.py:103
  42.5 10.8 %collective-permute-start.4 = (bf16[16,128,128]{2,1,0:T(8,128)(2,1)}, bf16[16,128,128]{2,1,0:T(8,128)(2,1)}, u32[]{:S(2)}, u32[]{:S(2)}) collective-permute-start(bf16[16,128,128]{2,1,0:T(8,128)(2,1)} %collective-permute-done.2), channel_id=1, source_target_pairs={{0,1},{1,2},{2,3},{3,4},{4,5},{5,6},{6,7},{7,0},{8,9},{9,10},{10,1... | collective-permute-start | bytes 1572872 | tf_op jit(solution)/shard_map/ppermute | solution.py:98
  43.8 17.0 %collective-permute-start.5 = (bf16[16,128,128]{2,1,0:T(8,128)(2,1)}, bf16[16,128,128]{2,1,0:T(8,128)(2,1)S(1)}, u32[]{:S(2)}, u32[]{:S(2)}) collective-permute-start(bf16[16,128,128]{2,1,0:T(8,128)(2,1)} %collective-permute-done.3), channel_id=1, source_target_pairs={{0,7},{1,0},{2,1},{3,2},{4,3},{5,4},{6,5},{7,6},{8,15},{9,8},{10,9... | collective-permute-start | bytes 1572872 | tf_op jit(solution)/shard_map/ppermute | solution.py:103
  53.3 11.9 %collective-permute-start.6 = (bf16[16,128,128]{2,1,0:T(8,128)(2,1)}, bf16[16,128,128]{2,1,0:T(8,128)(2,1)S(1)}, u32[]{:S(2)}, u32[]{:S(2)}) collective-permute-start(bf16[16,128,128]{2,1,0:T(8,128)(2,1)} %collective-permute-done.4), channel_id=1, source_target_pairs={{0,1},{1,2},{2,3},{3,4},{4,5},{5,6},{6,7},{7,0},{8,9},{9,10},{10,1... | collective-permute-start | bytes 1572872 | tf_op jit(solution)/shard_map/ppermute | solution.py:98
  222.2 411.6 %reduce-scatter.8.cloned.1.call-start = ((), (), s32[]{:S(2)}) async-start(), calls=%async_computation.6 | async-start | bytes 9437184 | tf_op jit(solution)/shard_map/reduce_scatter | solution.py:116
  339.2 294.5 %copy-start.2 = (f32[16,128,128]{2,1,0:T(8,128)}, f32[16,128,128]{2,1,0:T(8,128)S(1)}, u32[]{:S(2)}) copy-start(f32[16,128,128]{2,1,0:T(8,128)S(1)} %get-tuple-element.419) | copy-start | bytes 3145732
  339.2 13.8 %collective-permute-start.7 = (bf16[16,128,128]{2,1,0:T(8,128)(2,1)S(1)}, bf16[16,128,128]{2,1,0:T(8,128)(2,1)S(1)}, u32[]{:S(2)}, u32[]{:S(2)}) collective-permute-start(bf16[16,128,128]{2,1,0:T(8,128)(2,1)S(1)} %get-tuple-element.418), channel_id=1, source_target_pairs={{0,1},{1,2},{2,3},{3,4},{4,5},{5,6},{6,7},{7,0},{8,9},{9,10},{10,1... | collective-permute-start | bytes 1572872 | tf_op jit(solution)/shard_map/ppermute | solution.py:98
  339.2 13.8 %collective-permute-start.8 = (bf16[16,128,128]{2,1,0:T(8,128)(2,1)S(1)}, bf16[16,128,128]{2,1,0:T(8,128)(2,1)S(1)}, u32[]{:S(2)}, u32[]{:S(2)}) collective-permute-start(bf16[16,128,128]{2,1,0:T(8,128)(2,1)S(1)} %get-tuple-element.418), channel_id=1, source_target_pairs={{0,7},{1,0},{2,1},{3,2},{4,3},{5,4},{6,5},{7,6},{8,15},{9,8},{10,9... | collective-permute-start | bytes 1572872 | tf_op jit(solution)/shard_map/ppermute | solution.py:103
  353.0 12.6 %collective-permute-start.9 = (bf16[16,128,128]{2,1,0:T(8,128)(2,1)S(1)}, bf16[16,128,128]{2,1,0:T(8,128)(2,1)}, u32[]{:S(2)}, u32[]{:S(2)}) collective-permute-start(bf16[16,128,128]{2,1,0:T(8,128)(2,1)S(1)} %collective-permute-done.7), channel_id=1, source_target_pairs={{0,1},{1,2},{2,3},{3,4},{4,5},{5,6},{6,7},{7,0},{8,9},{9,10},{10,1... | collective-permute-start | bytes 1572872 | tf_op jit(solution)/shard_map/ppermute | solution.py:98
  353.8 13.1 %collective-permute-start.10 = (bf16[16,128,128]{2,1,0:T(8,128)(2,1)S(1)}, bf16[16,128,128]{2,1,0:T(8,128)(2,1)}, u32[]{:S(2)}, u32[]{:S(2)}) collective-permute-start(bf16[16,128,128]{2,1,0:T(8,128)(2,1)S(1)} %collective-permute-done.8), channel_id=1, source_target_pairs={{0,7},{1,0},{2,1},{3,2},{4,3},{5,4},{6,5},{7,6},{8,15},{9,8},{10,9... | collective-permute-start | bytes 1572872 | tf_op jit(solution)/shard_map/ppermute | solution.py:103
  365.6 12.7 %collective-permute-start.11 = (bf16[16,128,128]{2,1,0:T(8,128)(2,1)}, bf16[16,128,128]{2,1,0:T(8,128)(2,1)}, u32[]{:S(2)}, u32[]{:S(2)}) collective-permute-start(bf16[16,128,128]{2,1,0:T(8,128)(2,1)} %collective-permute-done.9), channel_id=1, source_target_pairs={{0,1},{1,2},{2,3},{3,4},{4,5},{5,6},{6,7},{7,0},{8,9},{9,10},{10,1... | collective-permute-start | bytes 1572872 | tf_op jit(solution)/shard_map/ppermute | solution.py:98
  367.0 17.9 %collective-permute-start.12 = (bf16[16,128,128]{2,1,0:T(8,128)(2,1)}, bf16[16,128,128]{2,1,0:T(8,128)(2,1)S(1)}, u32[]{:S(2)}, u32[]{:S(2)}) collective-permute-start(bf16[16,128,128]{2,1,0:T(8,128)(2,1)} %collective-permute-done.10), channel_id=1, source_target_pairs={{0,7},{1,0},{2,1},{3,2},{4,3},{5,4},{6,5},{7,6},{8,15},{9,8},{10,9... | collective-permute-start | bytes 1572872 | tf_op jit(solution)/shard_map/ppermute | solution.py:103
  378.3 10.6 %collective-permute-start.13 = (bf16[16,128,128]{2,1,0:T(8,128)(2,1)}, bf16[16,128,128]{2,1,0:T(8,128)(2,1)S(1)}, u32[]{:S(2)}, u32[]{:S(2)}) collective-permute-start(bf16[16,128,128]{2,1,0:T(8,128)(2,1)} %collective-permute-done.11), channel_id=1, source_target_pairs={{0,1},{1,2},{2,3},{3,4},{4,5},{5,6},{6,7},{7,0},{8,9},{9,10},{10,1... | collective-permute-start | bytes 1572872 | tf_op jit(solution)/shard_map/ppermute | solution.py:98
  546.0 406.7 %reduce-scatter.10.cloned.1.call-start = ((), (), s32[]{:S(2)}) async-start(), calls=%async_computation.7 | async-start | bytes 9437184 | tf_op jit(solution)/shard_map/reduce_scatter | solution.py:116
  658.1 13.8 %collective-permute-start.14 = (bf16[16,128,128]{2,1,0:T(8,128)(2,1)S(1)}, bf16[16,128,128]{2,1,0:T(8,128)(2,1)S(1)}, u32[]{:S(2)}, u32[]{:S(2)}) collective-permute-start(bf16[16,128,128]{2,1,0:T(8,128)(2,1)S(1)} %get-tuple-element.415), channel_id=1, source_target_pairs={{0,1},{1,2},{2,3},{3,4},{4,5},{5,6},{6,7},{7,0},{8,9},{9,10},{10,1... | collective-permute-start | bytes 1572872 | tf_op jit(solution)/shard_map/ppermute | solution.py:98
  658.1 13.8 %collective-permute-start.15 = (bf16[16,128,128]{2,1,0:T(8,128)(2,1)S(1)}, bf16[16,128,128]{2,1,0:T(8,128)(2,1)S(1)}, u32[]{:S(2)}, u32[]{:S(2)}) collective-permute-start(bf16[16,128,128]{2,1,0:T(8,128)(2,1)S(1)} %get-tuple-element.415), channel_id=1, source_target_pairs={{0,7},{1,0},{2,1},{3,2},{4,3},{5,4},{6,5},{7,6},{8,15},{9,8},{10,9... | collective-permute-start | bytes 1572872 | tf_op jit(solution)/shard_map/ppermute | solution.py:103
  671.9 12.6 %collective-permute-start.16 = (bf16[16,128,128]{2,1,0:T(8,128)(2,1)S(1)}, bf16[16,128,128]{2,1,0:T(8,128)(2,1)}, u32[]{:S(2)}, u32[]{:S(2)}) collective-permute-start(bf16[16,128,128]{2,1,0:T(8,128)(2,1)S(1)} %collective-permute-done.14), channel_id=1, source_target_pairs={{0,1},{1,2},{2,3},{3,4},{4,5},{5,6},{6,7},{7,0},{8,9},{9,10},{10,1... | collective-permute-start | bytes 1572872 | tf_op jit(solution)/shard_map/ppermute | solution.py:98
  672.6 13.1 %collective-permute-start.17 = (bf16[16,128,128]{2,1,0:T(8,128)(2,1)S(1)}, bf16[16,128,128]{2,1,0:T(8,128)(2,1)}, u32[]{:S(2)}, u32[]{:S(2)}) collective-permute-start(bf16[16,128,128]{2,1,0:T(8,128)(2,1)S(1)} %collective-permute-done.15), channel_id=1, source_target_pairs={{0,7},{1,0},{2,1},{3,2},{4,3},{5,4},{6,5},{7,6},{8,15},{9,8},{10,9... | collective-permute-start | bytes 1572872 | tf_op jit(solution)/shard_map/ppermute | solution.py:103
  684.4 12.7 %collective-permute-start.18 = (bf16[16,128,128]{2,1,0:T(8,128)(2,1)}, bf16[16,128,128]{2,1,0:T(8,128)(2,1)}, u32[]{:S(2)}, u32[]{:S(2)}) collective-permute-start(bf16[16,128,128]{2,1,0:T(8,128)(2,1)} %collective-permute-done.16), channel_id=1, source_target_pairs={{0,1},{1,2},{2,3},{3,4},{4,5},{5,6},{6,7},{7,0},{8,9},{9,10},{10,1... | collective-permute-start | bytes 1572872 | tf_op jit(solution)/shard_map/ppermute | solution.py:98
  685.8 17.9 %collective-permute-start.19 = (bf16[16,128,128]{2,1,0:T(8,128)(2,1)}, bf16[16,128,128]{2,1,0:T(8,128)(2,1)S(1)}, u32[]{:S(2)}, u32[]{:S(2)}) collective-permute-start(bf16[16,128,128]{2,1,0:T(8,128)(2,1)} %collective-permute-done.17), channel_id=1, source_target_pairs={{0,7},{1,0},{2,1},{3,2},{4,3},{5,4},{6,5},{7,6},{8,15},{9,8},{10,9... | collective-permute-start | bytes 1572872 | tf_op jit(solution)/shard_map/ppermute | solution.py:103
  697.1 10.6 %collective-permute-start.20 = (bf16[16,128,128]{2,1,0:T(8,128)(2,1)}, bf16[16,128,128]{2,1,0:T(8,128)(2,1)S(1)}, u32[]{:S(2)}, u32[]{:S(2)}) collective-permute-start(bf16[16,128,128]{2,1,0:T(8,128)(2,1)} %collective-permute-done.18), channel_id=1, source_target_pairs={{0,1},{1,2},{2,3},{3,4},{4,5},{5,6},{6,7},{7,0},{8,9},{9,10},{10,1... | collective-permute-start | bytes 1572872 | tf_op jit(solution)/shard_map/ppermute | solution.py:98
  864.8 142.8 %reduce-scatter.14.cloned.1.call-start = ((), (), s32[]{:S(2)}) async-start(), calls=%async_computation.9 | async-start | bytes 589824 | tf_op jit(solution)/shard_map/reduce_scatter | solution.py:134
  952.6 23.3 %copy-start.14 = (s32[16]{0:T(128)S(1)}, s32[16]{0:T(128)}, u32[]{:S(2)}) copy-start(s32[16]{0:T(128)} %copy-done.13) | copy-start | bytes 196
  978.0 61.1 %reduce-scatter.12.cloned.1.call-start = ((), (), s32[]{:S(2)}) async-start(), calls=%async_computation.8 | async-start | bytes 589824 | tf_op jit(solution)/shard_map/reduce_scatter | solution.py:133
  1007.6 31.5 %collective-permute-start.21 = (f32[128,128]{1,0:T(8,128)}, f32[128,128]{1,0:T(8,128)S(1)}, u32[]{:S(2)}, u32[]{:S(2)}) collective-permute-start(f32[128,128]{1,0:T(8,128)} %reduce-scatter.14.cloned.1.call-done), channel_id=1, source_target_pairs={{0,8},{8,16},{16,24},{1,9},{9,17},{17,25},{2,10},{10,18},{18,26},{... | collective-permute-start | bytes 196616 | tf_op jit(solution)/shard_map/ppermute | solution.py:16
  (10 other events, 29.5 us)
Sparse Core Ops, SparseCore 0:
  222.3 92.7 reduce-scatter.5
  546.1 87.6 reduce-scatter.7
  864.9 87.6 reduce-scatter.9
  978.1 29.4 reduce-scatter.13
  1009.7 29.3 reduce-scatter.11
